TPU v7x, 512 devices: a whole 4x4x16 slice. The times are simulated.
512 devices in a mesh: expert: 32 (over z, core), replica: 16 (over x, y).
Axes of the slice: x: 4, y: 4, z: 16, core: 2. Of those that a mesh axis runs over, the one named last changes fastest.
Arguments:
- weights: bfloat16 [32, 3, 2048, 512], P('expert', None, 'replica'), may hold values from -0.125 to 0.125
- first_moment: float32 [32, 3, 2048, 512], P('expert', None, 'replica'), may hold values from -128 to 128
- second_moment: float32 [32, 3, 2048, 512], P('expert', None, 'replica'), may hold values from 100 to 100000
- out_grads: bfloat16 [16, 4096, 2048], P('replica', 'expert'), may hold values from -8 to 8
- routes: int32 [16, 4096, 1], P('replica', 'expert'), may hold values from 0 to 31; in each aligned block of 128 rows (0 to 127, 128 to 255, ..., all dimensions but the last counted through in order) at most 8 rows name the same one
- task_ids: int32 [16, 32], P('replica', 'expert'), may hold values from 0 to 7
- task_weights: float32 [8], replicated, may hold values from 0.25 to 4
- saved_inputs: bfloat16 [16, 32, 256, 2048], P('replica', 'expert'), may hold values from -8 to 8
Outputs:
- input_grads: bfloat16 [16, 4096, 2048], P('replica', 'expert')
- adam_step: float32 [32, 3, 2048, 512], P('expert', None, 'replica')
Inputs may be any that keep to these rules, and one draw needn't show every extreme that they name: `routes`: at most 8 of the rows of one device go to one expert, and in every draw some device sends exactly 8 rows to some expert.
All inputs are finite; a program needn't handle non-finite values.
Results may differ from a plain program's by a relative error of at most 0.0057.
Values may be sent and summed in bfloat16 or wider, within the bound.
A program may use at most 128 MiB of HBM per device.

v0:
```python
import jax
import jax.numpy as jnp
from jax import lax
from jax.sharding import PartitionSpec as P

beta_first = 0.9
beta_second = 0.95
adam_eps = 1e-08
norm_eps = 1e-06
first_fix = 1.0 - (0.9**50) ** 2
second_fix = 1.0 - (0.95**50) ** 2


def from_partner(array, axis, bit):
    return lax.ppermute(array, axis, [(i, i ^ 1 << bit) for i in range(lax.axis_size(axis))])


def contract_rows(left, right):
    return lax.dot_general(
        left, right, (((0,), (0,)), ((), ())), preferred_element_type=jnp.float32
    )


def contract_last(left, right):
    return lax.dot_general(
        left, right, (((1,), (1,)), ((), ())), preferred_element_type=jnp.float32
    )


def group_total(partials, level_now):
    totals = partials
    for bit_pos in range(level_now + 1):
        totals = totals + from_partner(totals, "replica", bit_pos)
    return totals


def merge_level(kept_part, got_part, bit_now, level_now):
    own_square = jnp.sum(kept_part * kept_part)
    got_square = jnp.sum(got_part * got_part)
    cross_sum = jnp.sum(kept_part * got_part)
    low_side = bit_now == 0
    norm_first = jnp.where(low_side, own_square, got_square)
    norm_second = jnp.where(low_side, got_square, own_square)
    totals = group_total(jnp.stack([cross_sum, norm_first, norm_second]), level_now)
    coef_first = 1.0 - totals[0] / (2.0 * (totals[1] + norm_eps))
    coef_second = 1.0 - totals[0] / (2.0 * (totals[2] + norm_eps))
    kept_coef = jnp.where(low_side, coef_first, coef_second)
    got_coef = jnp.where(low_side, coef_second, coef_first)
    return kept_coef * kept_part + got_coef * got_part


def split_level(pieces, level_now, rep_index):
    bit_now = rep_index >> level_now & 1
    paired = pieces.reshape(
        pieces.shape[0], pieces.shape[1] // 2, 2, pieces.shape[2], pieces.shape[3]
    )
    kept_part = lax.dynamic_index_in_dim(paired, bit_now, axis=2, keepdims=False)
    give_part = lax.dynamic_index_in_dim(paired, 1 - bit_now, axis=2, keepdims=False)
    got_part = from_partner(give_part.astype(jnp.bfloat16), "replica", level_now).astype(
        jnp.float32
    )
    return merge_level(kept_part, got_part, bit_now, level_now)


def shards(
    weights, first_moment, second_moment, out_grads, routes, task_ids, task_weights, saved_inputs
):
    expert_count = lax.axis_size("expert")
    rep_count = lax.axis_size("replica")
    rep_index = lax.axis_index("replica")
    row_count = out_grads.shape[1]
    model_width = out_grads.shape[2]
    hidden_width = weights.shape[3]
    slot_count = saved_inputs.shape[2]
    capacity = slot_count // expert_count
    block_count = task_ids.shape[1]
    block_rows = row_count // block_count
    task_count = task_weights.shape[0]
    seg_rows = model_width // rep_count
    levels = rep_count.bit_length() - 1
    chosen_task = (task_ids[0][:, None] == jnp.arange(task_count, dtype=jnp.int32)[None, :]).astype(
        jnp.float32
    )
    block_weight = jnp.sum(chosen_task * task_weights[None, :], axis=1)
    scaled = (
        (out_grads[0].reshape(block_count, block_rows, model_width) * block_weight[:, None, None])
        .reshape(row_count, model_width)
        .astype(jnp.bfloat16)
    )
    expert_of = routes[0, :, 0]
    chosen = (expert_of[:, None] == jnp.arange(expert_count, dtype=jnp.int32)[None, :]).astype(
        jnp.int32
    )
    slot_rank = jnp.sum((jnp.cumsum(chosen, axis=0) - chosen) * chosen, axis=1)
    slot_index = expert_of * capacity + slot_rank
    placing = (slot_index[:, None] == jnp.arange(slot_count, dtype=jnp.int32)[None, :]).astype(
        jnp.bfloat16
    )
    outgoing = (
        contract_rows(placing, scaled)
        .astype(jnp.bfloat16)
        .reshape(expert_count, capacity, model_width)
    )
    incoming = lax.all_to_all(outgoing, "expert", split_axis=0, concat_axis=0, tiled=True).reshape(
        slot_count, model_width
    )
    gathered = lax.all_gather(weights, "replica", axis=2, tiled=True)[0]
    inputs = saved_inputs[0, 0]
    gate_pre = jnp.dot(inputs, gathered[0], preferred_element_type=jnp.float32)
    up_pre = jnp.dot(inputs, gathered[1], preferred_element_type=jnp.float32)
    gate_act = jax.nn.silu(gate_pre)
    hidden = (gate_act * up_pre).astype(jnp.bfloat16)
    hidden_grad = jnp.dot(incoming, gathered[2], preferred_element_type=jnp.float32)
    sigmoid_gate = jax.nn.sigmoid(gate_pre)
    gate_grad = (
        hidden_grad * up_pre * sigmoid_gate * (1.0 + gate_pre * (1.0 - sigmoid_gate))
    ).astype(jnp.bfloat16)
    up_grad = (hidden_grad * gate_act).astype(jnp.bfloat16)
    slot_grads = (
        contract_last(gate_grad, gathered[0]) + contract_last(up_grad, gathered[1])
    ).astype(jnp.bfloat16)
    returned = lax.all_to_all(
        slot_grads.reshape(expert_count, capacity, model_width),
        "expert",
        split_axis=0,
        concat_axis=0,
        tiled=True,
    ).reshape(slot_count, model_width)
    input_grads = jnp.dot(placing, returned, preferred_element_type=jnp.float32).astype(
        jnp.bfloat16
    )[None]
    pieces = jnp.stack(
        [
            contract_rows(inputs, gate_grad),
            contract_rows(inputs, up_grad),
            contract_rows(incoming, hidden),
        ]
    )
    pieces = pieces.reshape(3, rep_count, seg_rows, hidden_width)
    start_level = 0
    for level_now in range(start_level, levels):
        pieces = split_level(pieces, level_now, rep_index)
    merged = pieces.reshape(3, seg_rows, hidden_width)
    first_new = beta_first * first_moment[0] + (1.0 - beta_first) * merged
    second_new = beta_second * second_moment[0] + (1.0 - beta_second) * merged * merged
    adam_step = (first_new / first_fix / (jnp.sqrt(second_new / second_fix) + adam_eps))[None]
    return (input_grads, adam_step)


def solution(mesh):
    return jax.shard_map(
        shards,
        mesh=mesh,
        in_specs=(
            P("expert", None, "replica", None),
            P("expert", None, "replica", None),
            P("expert", None, "replica", None),
            P("replica", "expert", None),
            P("replica", "expert", None),
            P("replica", "expert"),
            P(),
            P("replica", "expert", None, None),
        ),
        out_specs=(P("replica", "expert", None), P("expert", None, "replica", None)),
        check_vma=False,
    )
```

profile of v0, /device:TPU:6, one launch (start us, length us, event | category | flops | bytes accessed | tf_op | source)
XLA Modules:
  0.0 398.2 jit_solution(11649684531243421679)
XLA Ops:
  8.6 0.7 fusion.46
  9.5 1.3 fusion.47
  10.7 0.8 select_reduce_fusion
  12.2 3.2 fusion.10
  15.5 15.5 %all-to-all-start = ((bf16[32,8,2048]{2,1,0:T(8,128)(2,1)}), bf16[32,8,2048]{2,1,0:T(8,128)(2,1)S(1)}, u32[]{:S(2)}, u32[]{:S(2)}) async-start(bf16[32,8,2048]{2,1,0:T(8,128)(2,1)} %fusion.10), calls=%async_computation | async-start | bytes 2097152 | tf_op jit(solution)/shard_map/all_to_all | solution.py:104
  31.0 56.0 %all-to-all-done = bf16[32,8,2048]{2,1,0:T(8,128)(2,1)S(1)} async-done(((bf16[32,8,2048]{2,1,0:T(8,128)(2,1)}), bf16[32,8,2048]{2,1,0:T(8,128)(2,1)S(1)}, u32[]{:S(2)}, u32[]{:S(2)}) %all-to-all-start) | async-done | bytes 1048608 | tf_op jit(solution)/shard_map/all_to_all | solution.py:104
  87.5 4.4 %all-gather.2.cloned.1.call-done = bf16[1,3,2048,512]{3,2,1,0:T(8,128)(2,1)} async-done(((bf16[1,3,128,512]{3,2,1,0:T(8,128)(2,1)}), bf16[1,3,2048,512]{3,2,1,0:T(8,128)(2,1)}) %all-gather.2.cloned.1.call-update) | async-done | bytes 6291472 | tf_op jit(solution)/shard_map/all_gather | solution.py:107
  91.9 2.3 fusion.16
  94.2 2.3 fusion.14
  96.5 2.9 convolution_bitcast_fusion.2
  99.3 2.4 multiply_convert_fusion.2
  101.8 2.7 convolution_bitcast_fusion
  104.4 5.3 %copy.19 = f32[2048,512]{1,0:T(8,128)} copy(f32[2048,512]{0,1:T(8,128)} %convolution_bitcast_fusion) | data formatting | bytes 8388608 | tf_op jit(solution)/shard_map/stack | solution.py:132
  109.8 2.7 convolution_bitcast_fusion.1
  112.4 5.3 %copy.18 = f32[2048,512]{1,0:T(8,128)} copy(f32[2048,512]{0,1:T(8,128)} %convolution_bitcast_fusion.1) | data formatting | bytes 8388608 | tf_op jit(solution)/shard_map/stack | solution.py:132
  117.8 11.9 %pad_maximum_fusion = f32[3,8,2,128,512]{4,3,2,1,0:T(8,128)} fusion(f32[1,8,2,128,512]{4,3,2,1,0:T(8,128)} %convolution_bitcast_fusion.2, f32[1,8,2,128,512]{4,3,2,1,0:T(8,128)} %bitcast.127, f32[1,8,2,128,512]{4,3,2,1,0:T(8,128)} %bitcast.128), kind=kLoop, calls=%fused_computation | loop fusion | flops 6291456 | bytes 25165824 | tf_op jit(solution)/shard_map/stack | solution.py:132
  129.7 4.9 %fusion.7 = bf16[3,8,128,512]{3,2,1,0:T(8,128)(2,1)} fusion(f32[3,8,2,128,512]{4,3,2,1,0:T(8,128)} %pad_maximum_fusion, s32[]{:T(128)S(6)} %select_n.78), kind=kLoop, calls=%fused_computation.19 | loop fusion | bytes 6291460 | tf_op jit(solution)/shard_map/convert_element_type | solution.py:59
  134.6 2.1 collective-permute-start
  136.7 69.7 %collective-permute-done = bf16[3,8,128,512]{3,2,1,0:T(8,128)(2,1)} collective-permute-done((bf16[3,8,128,512]{3,2,1,0:T(8,128)(2,1)}, bf16[3,8,128,512]{3,2,1,0:T(8,128)(2,1)}, u32[]{:S(2)}, u32[]{:S(2)}) %collective-permute-start) | collective-permute-done | bytes 3145760 | tf_op jit(solution)/shard_map/ppermute | solution.py:15
  206.4 6.0 %fusion = (f32[]{:T(128)}, f32[]{:T(128)}, f32[]{:T(128)}) fusion(bf16[3,8,128,512]{3,2,1,0:T(8,128)(2,1)} %collective-permute-done, f32[3,8,2,128,512]{4,3,2,1,0:T(8,128)} %pad_maximum_fusion, s32[]{:T(128)S(6)} %select_n.77), kind=kLoop, calls=%fused_computation.4 | loop fusion | flops 11010045 | bytes 9437200 | tf_op jit(solution)/shard_map/reduce_sum | solution.py:40
  215.1 0.7 pad_maximum_fusion.1
  215.8 2.2 collective-permute-start.1
  218.0 3.3 collective-permute-done.1
  225.2 5.2 %fusion.2 = f32[3,8,128,512]{3,2,1,0:T(8,128)S(1)} fusion(bf16[3,8,128,512]{3,2,1,0:T(8,128)(2,1)} %collective-permute-done, f32[3,8,2,128,512]{4,3,2,1,0:T(8,128)} %pad_maximum_fusion, s32[]{:T(128)S(6)} %select_n.77, f32[]{:T(128)S(6)} %select_n.82, f32[]{:T(128)S(6)} %select_n.81), kind=kLoop, calls=%fused_computation.6 | loop fusion | flops 6291456 | bytes 15728652 | tf_op jit(solution)/shard_map/add | solution.py:49
  230.5 1.5 fusion.20
  232.0 3.5 collective-permute-start.2
  235.6 2.3 fusion.15
  237.9 3.4 fusion.11
  241.3 12.7 %all-to-all-start.1 = ((bf16[32,8,2048]{2,1,0:T(8,128)(2,1)}), bf16[32,8,2048]{2,1,0:T(8,128)(2,1)}, u32[]{:S(2)}, u32[]{:S(2)}) async-start(bf16[32,8,2048]{2,1,0:T(8,128)(2,1)} %fusion.11), calls=%async_computation.1 | async-start | bytes 2097152 | tf_op jit(solution)/shard_map/all_to_all | solution.py:122
  254.0 15.5 %collective-permute-done.2 = bf16[3,4,128,512]{3,2,1,0:T(8,128)(2,1)S(1)} collective-permute-done((bf16[3,4,128,512]{3,2,1,0:T(8,128)(2,1)}, bf16[3,4,128,512]{3,2,1,0:T(8,128)(2,1)S(1)}, u32[]{:S(2)}, u32[]{:S(2)}) %collective-permute-start.2) | collective-permute-done | bytes 1572896 | tf_op jit(solution)/shard_map/ppermute | solution.py:15
  269.6 3.3 fusion.4
  275.3 0.7 pad_maximum_fusion.2
  276.1 2.3 collective-permute-start.3
  278.3 3.2 collective-permute-done.3
  282.2 3.4 collective-permute-start.4
  285.6 3.6 collective-permute-done.4
  289.2 0.7 fusion.65
  293.0 2.5 fusion.6
  295.5 1.7 copy-done.3
  297.2 2.8 collective-permute-start.5
  300.0 14.0 %collective-permute-done.5 = bf16[3,2,128,512]{3,2,1,0:T(8,128)(2,1)S(1)} collective-permute-done((bf16[3,2,128,512]{3,2,1,0:T(8,128)(2,1)S(1)}, bf16[3,2,128,512]{3,2,1,0:T(8,128)(2,1)S(1)}, u32[]{:S(2)}, u32[]{:S(2)}) %collective-permute-start.5) | collective-permute-done | bytes 786464 | tf_op jit(solution)/shard_map/ppermute | solution.py:15
  314.0 2.4 fusion.17
  318.8 0.7 pad_maximum_fusion.3
  319.5 2.2 collective-permute-start.6
  321.7 3.3 collective-permute-done.6
  325.7 3.4 collective-permute-start.7
  329.1 3.6 collective-permute-done.7
  333.4 2.7 collective-permute-start.8
  336.1 2.7 collective-permute-done.8
  341.8 1.7 fusion.19
  343.6 3.4 collective-permute-start.9
  347.0 2.5 fusion.12
  349.5 5.3 %collective-permute-done.9 = bf16[3,1,128,512]{3,2,1,0:T(8,128)(2,1)S(1)} collective-permute-done((bf16[3,1,128,512]{3,2,1,0:T(8,128)(2,1)S(1)}, bf16[3,1,128,512]{3,2,1,0:T(8,128)(2,1)S(1)}, u32[]{:S(2)}, u32[]{:S(2)}) %collective-permute-start.9) | collective-permute-done | bytes 393248 | tf_op jit(solution)/shard_map/ppermute | solution.py:15
  354.8 0.9 fusion.27
  358.2 0.7 pad_maximum_fusion.4
  358.9 2.2 collective-permute-start.10
  361.1 3.3 collective-permute-done.10
  365.1 3.4 collective-permute-start.11
  368.5 3.6 collective-permute-done.11
  372.8 2.7 collective-permute-start.12
  375.5 2.7 collective-permute-done.12
  378.2 3.4 collective-permute-start.13
  381.6 3.6 collective-permute-done.13
  388.5 2.9 fusion.35
  (28 shorter events, 9.1 us)
Async XLA Ops:
  7.2 84.7 %copy-start = (bf16[1,1,256,2048]{3,2,1,0:T(8,128)(2,1)S(1)}, bf16[1,1,256,2048]{3,2,1,0:T(8,128)(2,1)}, u32[]{:S(2)}) copy-start(bf16[1,1,256,2048]{3,2,1,0:T(8,128)(2,1)} %param.15) | copy-start | bytes 3145732
  7.2 84.7 %all-gather.2.cloned.1.call-start = ((), (), s32[]{:S(2)}) async-start(), calls=%async_computation.2 | async-start | bytes 6684672 | tf_op jit(solution)/shard_map/all_gather | solution.py:107
  15.5 71.5 %all-to-all-start = ((bf16[32,8,2048]{2,1,0:T(8,128)(2,1)}), bf16[32,8,2048]{2,1,0:T(8,128)(2,1)S(1)}, u32[]{:S(2)}, u32[]{:S(2)}) async-start(bf16[32,8,2048]{2,1,0:T(8,128)(2,1)} %fusion.10), calls=%async_computation | async-start | bytes 2097152 | tf_op jit(solution)/shard_map/all_to_all | solution.py:104
  134.6 71.9 %collective-permute-start = (bf16[3,8,128,512]{3,2,1,0:T(8,128)(2,1)}, bf16[3,8,128,512]{3,2,1,0:T(8,128)(2,1)}, u32[]{:S(2)}, u32[]{:S(2)}) collective-permute-start(bf16[3,8,128,512]{3,2,1,0:T(8,128)(2,1)} %fusion.7), channel_id=1, source_target_pairs={{0,1},{1,0},{2,3},{3,2},{4,5},{5,4},{6,7},{7,6},{8,9},{9,8},{10,11... | collective-permute-start | bytes 9437192 | tf_op jit(solution)/shard_map/ppermute | solution.py:15
  215.8 5.5 %collective-permute-start.1 = (f32[3]{0:T(128)S(1)}, f32[3]{0:T(128)S(1)}, u32[]{:S(2)}, u32[]{:S(2)}) collective-permute-start(f32[3]{0:T(128)S(1)} %pad_maximum_fusion.1), channel_id=1, source_target_pairs={{0,1},{1,0},{2,3},{3,2},{4,5},{5,4},{6,7},{7,6},{8,9},{9,8},{10,11... | collective-permute-start | bytes 44 | tf_op jit(solution)/shard_map/ppermute | solution.py:15
  230.5 7.4 %copy-start.2 = (f32[3,8,128,512]{3,2,1,0:T(8,128)}, f32[3,8,128,512]{3,2,1,0:T(8,128)S(1)}, u32[]{:S(2)}) copy-start(f32[3,8,128,512]{3,2,1,0:T(8,128)S(1)} %fusion.2) | copy-start | bytes 18874372
  232.0 37.6 %collective-permute-start.2 = (bf16[3,4,128,512]{3,2,1,0:T(8,128)(2,1)}, bf16[3,4,128,512]{3,2,1,0:T(8,128)(2,1)S(1)}, u32[]{:S(2)}, u32[]{:S(2)}) collective-permute-start(bf16[3,4,128,512]{3,2,1,0:T(8,128)(2,1)} %fusion.20), channel_id=1, source_target_pairs={{0,2},{1,3},{2,0},{3,1},{4,6},{5,7},{6,4},{7,5},{8,10},{9,11},{10,... | collective-permute-start | bytes 4718600 | tf_op jit(solution)/shard_map/ppermute | solution.py:15
  241.3 105.7 %all-to-all-start.1 = ((bf16[32,8,2048]{2,1,0:T(8,128)(2,1)}), bf16[32,8,2048]{2,1,0:T(8,128)(2,1)}, u32[]{:S(2)}, u32[]{:S(2)}) async-start(bf16[32,8,2048]{2,1,0:T(8,128)(2,1)} %fusion.11), calls=%async_computation.1 | async-start | bytes 2097152 | tf_op jit(solution)/shard_map/all_to_all | solution.py:122
  276.1 5.5 %collective-permute-start.3 = (f32[3]{0:T(128)S(1)}, f32[3]{0:T(128)S(1)}, u32[]{:S(2)}, u32[]{:S(2)}) collective-permute-start(f32[3]{0:T(128)S(1)} %pad_maximum_fusion.2), channel_id=1, source_target_pairs={{0,1},{1,0},{2,3},{3,2},{4,5},{5,4},{6,7},{7,6},{8,9},{9,8},{10,11... | collective-permute-start | bytes 44 | tf_op jit(solution)/shard_map/ppermute | solution.py:15
  282.2 7.0 %collective-permute-start.4 = (f32[3]{0:T(128)S(1)}, f32[3]{0:T(128)S(1)}, u32[]{:S(2)}, u32[]{:S(2)}) collective-permute-start(f32[3]{0:T(128)S(1)} %fusion.61), channel_id=1, source_target_pairs={{0,2},{1,3},{2,0},{3,1},{4,6},{5,7},{6,4},{7,5},{8,10},{9,11},{10,... | collective-permute-start | bytes 44 | tf_op jit(solution)/shard_map/ppermute | solution.py:15
  295.5 1.7 copy-start.3
  297.2 16.7 %collective-permute-start.5 = (bf16[3,2,128,512]{3,2,1,0:T(8,128)(2,1)S(1)}, bf16[3,2,128,512]{3,2,1,0:T(8,128)(2,1)S(1)}, u32[]{:S(2)}, u32[]{:S(2)}) collective-permute-start(bf16[3,2,128,512]{3,2,1,0:T(8,128)(2,1)S(1)} %fusion.36), channel_id=1, source_target_pairs={{0,4},{1,5},{2,6},{3,7},{4,0},{5,1},{6,2},{7,3},{8,12},{9,13},{10,... | collective-permute-start | bytes 2359304 | tf_op jit(solution)/shard_map/ppermute | solution.py:15
  319.5 5.5 %collective-permute-start.6 = (f32[3]{0:T(128)S(1)}, f32[3]{0:T(128)S(1)}, u32[]{:S(2)}, u32[]{:S(2)}) collective-permute-start(f32[3]{0:T(128)S(1)} %pad_maximum_fusion.3), channel_id=1, source_target_pairs={{0,1},{1,0},{2,3},{3,2},{4,5},{5,4},{6,7},{7,6},{8,9},{9,8},{10,11... | collective-permute-start | bytes 44 | tf_op jit(solution)/shard_map/ppermute | solution.py:15
  325.7 7.0 %collective-permute-start.7 = (f32[3]{0:T(128)S(1)}, f32[3]{0:T(128)S(1)}, u32[]{:S(2)}, u32[]{:S(2)}) collective-permute-start(f32[3]{0:T(128)S(1)} %fusion.60), channel_id=1, source_target_pairs={{0,2},{1,3},{2,0},{3,1},{4,6},{5,7},{6,4},{7,5},{8,10},{9,11},{10,... | collective-permute-start | bytes 44 | tf_op jit(solution)/shard_map/ppermute | solution.py:15
  333.4 5.5 %collective-permute-start.8 = (f32[3]{0:T(128)S(1)}, f32[3]{0:T(128)S(1)}, u32[]{:S(2)}, u32[]{:S(2)}) collective-permute-start(f32[3]{0:T(128)S(1)} %fusion.64), channel_id=1, source_target_pairs={{0,4},{1,5},{2,6},{3,7},{4,0},{5,1},{6,2},{7,3},{8,12},{9,13},{10,... | collective-permute-start | bytes 44 | tf_op jit(solution)/shard_map/ppermute | solution.py:15
  343.6 11.2 %collective-permute-start.9 = (bf16[3,1,128,512]{3,2,1,0:T(8,128)(2,1)S(1)}, bf16[3,1,128,512]{3,2,1,0:T(8,128)(2,1)S(1)}, u32[]{:S(2)}, u32[]{:S(2)}) collective-permute-start(bf16[3,1,128,512]{3,2,1,0:T(8,128)(2,1)S(1)} %dynamic-slice_convert_fusion.2), channel_id=1, source_target_pairs={{0,8},{1,9},{2,10},{3,11},{4,12},{5,13},{6,14},{7,15},{8,0},{9,1},... | collective-permute-start | bytes 1179656 | tf_op jit(solution)/shard_map/ppermute | solution.py:15
  347.0 44.3 %copy-start.1 = (bf16[1,1,256,2048]{3,2,1,0:T(8,128)(2,1)S(1)}, bf16[1,1,256,2048]{3,2,1,0:T(8,128)(2,1)}, u32[]{:S(2)}) copy-start(bf16[1,1,256,2048]{3,2,1,0:T(8,128)(2,1)} %param.15) | copy-start | bytes 3145732
  358.9 5.5 %collective-permute-start.10 = (f32[3]{0:T(128)S(1)}, f32[3]{0:T(128)S(1)}, u32[]{:S(2)}, u32[]{:S(2)}) collective-permute-start(f32[3]{0:T(128)S(1)} %pad_maximum_fusion.4), channel_id=1, source_target_pairs={{0,1},{1,0},{2,3},{3,2},{4,5},{5,4},{6,7},{7,6},{8,9},{9,8},{10,11... | collective-permute-start | bytes 44 | tf_op jit(solution)/shard_map/ppermute | solution.py:15
  365.1 7.0 %collective-permute-start.11 = (f32[3]{0:T(128)S(1)}, f32[3]{0:T(128)S(1)}, u32[]{:S(2)}, u32[]{:S(2)}) collective-permute-start(f32[3]{0:T(128)S(1)} %fusion.59), channel_id=1, source_target_pairs={{0,2},{1,3},{2,0},{3,1},{4,6},{5,7},{6,4},{7,5},{8,10},{9,11},{10,... | collective-permute-start | bytes 44 | tf_op jit(solution)/shard_map/ppermute | solution.py:15
  372.8 5.5 %collective-permute-start.12 = (f32[3]{0:T(128)S(1)}, f32[3]{0:T(128)S(1)}, u32[]{:S(2)}, u32[]{:S(2)}) collective-permute-start(f32[3]{0:T(128)S(1)} %fusion.63), channel_id=1, source_target_pairs={{0,4},{1,5},{2,6},{3,7},{4,0},{5,1},{6,2},{7,3},{8,12},{9,13},{10,... | collective-permute-start | bytes 44 | tf_op jit(solution)/shard_map/ppermute | solution.py:15
  378.2 7.0 %collective-permute-start.13 = (f32[3]{0:T(128)S(1)}, f32[3]{0:T(128)S(1)}, u32[]{:S(2)}, u32[]{:S(2)}) collective-permute-start(f32[3]{0:T(128)S(1)} %add.168), channel_id=1, source_target_pairs={{0,8},{1,9},{2,10},{3,11},{4,12},{5,13},{6,14},{7,15},{8,0},{9,1},... | collective-permute-start | bytes 44 | tf_op jit(solution)/shard_map/ppermute | solution.py:15
Sparse Core Ops, SparseCore 0:
  11.1 80.7 all-gather.1
where the time goes:
time: 400 us; the launch traced here: 398 us
  waiting for transfers between devices  198 us (50%)
  starting transfers between devices  67.8 us (17%)
  other arithmetic  48.5 us (12%)
  between operations  35 us (9%)
  matrix products  26.6 us (7%)
  local copies, waits for them, and re-layouts  22 us (6%)
    ppermute x14, waiting for transfers between devices, from_partner(): lax.ppermute(array, axis, [(i, i ^ 1 << bit) for i in range(lax.axis_size...  137 us
    all_to_all x1, waiting for transfers between devices, shards(): lax.all_to_all(outgoing, 'expert', split_axis=0, concat_axis=0, tiled=True)  56 us
    ppermute x14, starting transfers between devices, from_partner(): lax.ppermute(array, axis, [(i, i ^ 1 << bit) for i in range(lax.axis_size...  39.6 us
    all_to_all x1, starting transfers between devices, shards(): lax.all_to_all(outgoing, 'expert', split_axis=0, concat_axis=0, tiled=True)  15.5 us
    all_to_all x1, starting transfers between devices, shards(): lax.all_to_all(slot_grads.reshape(expert_count, capacity, model_width), '...  12.7 us
    reduce_sum x4, other arithmetic, merge_level(): cross_sum = jnp.sum(kept_part * got_part)  12.7 us
    another operation x1, other arithmetic, shards(): jnp.stack([contract_rows(inputs, gate_grad), contract_rows(inputs, up_gra...  11.9 us
    dot_general x4, matrix products, contract_rows(): lax.dot_general(left, right, (((0,), (0,)), ((), ())), preferred_element_...  11.4 us
  transfers between devices with their start and end apart: 17, of which 16 were waited for; matrix products, arithmetic and copies ran while one was open for 8% of the time, Pallas kernels for 0%

commit v1 on v0

v1 whole, which is shorter than its diff:
```python
import functools

import jax
import jax.numpy as jnp
from jax import lax
from jax.experimental import pallas as pl
from jax.experimental.pallas import tpu as pltpu
from jax.sharding import PartitionSpec as P

beta_first = 0.9
beta_second = 0.95
adam_eps = 1e-08
norm_eps = 1e-06
first_fix = 1.0 - (0.9**50) ** 2
second_fix = 1.0 - (0.95**50) ** 2

F32 = jnp.float32
BF16 = jnp.bfloat16


def dot_rows(left, right):
    return lax.dot_general(left, right, (((0,), (0,)), ((), ())), preferred_element_type=F32)


def dot_last(left, right):
    return lax.dot_general(left, right, (((1,), (1,)), ((), ())), preferred_element_type=F32)


def iota(shape, axis):
    return lax.broadcasted_iota(jnp.int32, shape, axis)


def kernel(
    experts, nx, ny,
    w_ref, fm_ref, sm_ref, og_ref, route_ref, tid_ref, tw_ref, x_ref,
    ig_ref, step_ref,
    place, out3, in3, ret3, back3, rows, wfull, gact, upfac, gg, ug, hid, vsend, vbuf, acc, gsend, gbuf,
    a_send, a_recv, b_send, b_recv, w_send, w_recv, v_send, v_recv, g_send, g_recv,
):
    reps = nx * ny
    me_e = lax.axis_index("expert")
    me_r = lax.axis_index("replica")
    mx, my = me_r // ny, me_r % ny
    row_count, width = og_ref.shape
    slots = x_ref.shape[0]
    cap = slots // experts
    hidden = w_ref.shape[2]
    seg = w_ref.shape[1]
    half = seg // 2

    barrier = pltpu.get_barrier_semaphore()

    @pl.loop(1, experts)
    def _(i):
        pl.semaphore_signal(barrier, inc=1, device_id={"expert": (me_e + i) % experts, "replica": me_r})

    @pl.loop(1, reps)
    def _(i):
        pl.semaphore_signal(barrier, inc=1, device_id={"expert": me_e, "replica": (me_r + i) % reps})

    scale = tw_ref[tid_ref[0, 0]]
    expert_of = route_ref[...]
    chosen = (iota((experts, row_count), 0) == expert_of).astype(F32)
    earlier = (iota((row_count, row_count), 0) < iota((row_count, row_count), 1)).astype(BF16)
    before = jnp.dot(chosen.astype(BF16), earlier, preferred_element_type=F32)
    rank = jnp.sum(before * chosen, axis=0, keepdims=True)
    slot = expert_of * cap + rank.astype(jnp.int32)
    place[...] = (iota((slots, row_count), 0) == slot).astype(BF16)
    cols = min(512, width)
    for c in range(0, width, cols):
        scaled = (og_ref[:, c : c + cols].astype(F32) * scale).astype(BF16)
        moved = jnp.dot(place[...], scaled, preferred_element_type=F32)
        out3[:, :, c : c + cols] = moved.reshape(experts, cap, cols).astype(BF16)

    wfull[:, mx, my] = w_ref[...]
    pl.semaphore_wait(barrier, experts - 1 + reps - 1)

    def stage_one(k, along_y):
        lo = 0 if along_y else half
        idx = (0 if along_y else ny - 1) + k - 1
        to = mx * ny + (my + k) % ny if along_y else ((mx + k) % nx) * ny + my
        part = wfull.at[:, mx, my, lo : lo + half]
        return pltpu.make_async_remote_copy(
            src_ref=w_ref.at[:, lo : lo + half], dst_ref=part, send_sem=w_send.at[idx], recv_sem=w_recv.at[idx],
            device_id={"expert": me_e, "replica": to},
        )

    def stage_two(k, along_y, group):
        lo = half if along_y else 0
        base = (ny - 1) + (nx - 1)
        idx = base + (0 if along_y else ny - 1) + k - 1 + group * base
        to = mx * ny + (my + k) % ny if along_y else ((mx + k) % nx) * ny + my
        mats = pl.ds(0, 2) if group == 0 else pl.ds(2, 1)
        if along_y:
            part = wfull.at[mats, :, my, lo : lo + half]
        else:
            part = wfull.at[mats, mx, :, lo : lo + half]
        return pltpu.make_async_remote_copy(
            src_ref=part, dst_ref=part, send_sem=w_send.at[idx], recv_sem=w_recv.at[idx],
            device_id={"expert": me_e, "replica": to},
        )

    ones = [stage_one(k, True) for k in range(1, ny)] + [stage_one(k, False) for k in range(1, nx)]
    for c in ones:
        c.start()

    def row_copy(i, src, dst, send, recv):
        to = (me_e + i) % experts
        return pltpu.make_async_remote_copy(
            src_ref=src.at[to], dst_ref=dst.at[me_e], send_sem=send.at[i], recv_sem=recv.at[i],
            device_id={"expert": to, "replica": me_r},
        )

    def row_order(n):
        return (n + experts // 2) % experts

    @pl.loop(0, experts)
    def _(n):
        i = row_order(n)

        @pl.when(i != 0)
        def _():
            row_copy(i, out3, in3, a_send, a_recv).start()

    in3[me_e] = out3[me_e]

    for c in ones:
        c.wait_recv()
    twos = [
        [stage_two(k, True, g) for k in range(1, ny)] + [stage_two(k, False, g) for k in range(1, nx)]
        for g in range(2)
    ]
    for g in range(2):
        for c in twos[g]:
            c.start()

    for c in twos[0]:
        c.wait_recv()

    def weight(i):
        return wfull[i].reshape(reps * seg, hidden)

    xs = x_ref[...]
    gact[...] = jnp.dot(xs, weight(0), preferred_element_type=F32)
    upfac[...] = jnp.dot(xs, weight(1), preferred_element_type=F32)
    step_rows = 16

    @pl.loop(0, slots // step_rows)
    def _(n):
        at = pl.ds(pl.multiple_of(n * step_rows, step_rows), step_rows)
        gate, up = gact[at], upfac[at]
        sig = jax.nn.sigmoid(gate)
        act = gate * sig
        hid[at] = (act * up).astype(BF16)
        upfac[at] = up * sig * (1.0 + gate * (1.0 - sig))
        gact[at] = act

    for c in twos[1]:
        c.wait_recv()

    @pl.loop(1, experts)
    def _(i):
        row_copy(i, out3, in3, a_send, a_recv).wait_recv()

    def flat_rows(src):
        @pl.loop(0, slots // 16)
        def _(n):
            per = 16 // cap
            got = src[pl.ds(n * per, per)].astype(F32).reshape(16, width)
            rows[pl.ds(pl.multiple_of(n * 16, 16), 16)] = got.astype(BF16)

    flat_rows(in3)
    gact_now = jnp.dot(rows[...], weight(2), preferred_element_type=F32)
    gg[...] = (gact_now * upfac[...]).astype(BF16)
    ug[...] = (gact_now * gact[...]).astype(BF16)

    def offsets(k):
        i, j = k // ny, k % ny
        return (nx // 2 + (nx - 1) * i) % nx, (ny // 2 + (ny - 1) * j) % ny

    own_k = (nx // 2) * ny + ny // 2

    def seg_copy(k):
        dx, dy = offsets(k)
        to = ((mx + dx) % nx) * ny + (my + dy) % ny
        return pltpu.make_async_remote_copy(
            src_ref=vsend.at[to], dst_ref=vbuf.at[me_r], send_sem=v_send.at[k], recv_sem=v_recv.at[k],
            device_id={"expert": me_e, "replica": to},
        )

    def make_segment(k):
        dx, dy = offsets(k)
        to = ((mx + dx) % nx) * ny + (my + dy) % ny
        at = pl.ds(pl.multiple_of(to * seg, seg), seg)
        x_part = x_ref[:, at]
        vsend[to, 0:seg] = dot_rows(x_part, gg[...]).astype(BF16)
        vsend[to, seg : 2 * seg] = dot_rows(x_part, ug[...]).astype(BF16)
        vsend[to, 2 * seg : 3 * seg] = dot_rows(rows[:, at], hid[...]).astype(BF16)

        @pl.when(k != own_k)
        def _():
            seg_copy(k).start()

        @pl.when(k == own_k)
        def _():
            vbuf[me_r] = vsend[me_r]

    first_part = max(1, reps // 4)
    pl.loop(0, first_part)(make_segment)

    per = min(2, reps)

    @pl.loop(0, reps // per)
    def _(n):
        g_part = wfull[0, n * per // ny, pl.ds((n * per) % ny, per)].reshape(per * seg, hidden)
        u_part = wfull[1, n * per // ny, pl.ds((n * per) % ny, per)].reshape(per * seg, hidden)
        total = dot_last(gg[...], g_part) + dot_last(ug[...], u_part)
        at = pl.ds(pl.multiple_of(n * per * seg, per * seg), per * seg)
        ret3[:, :, at] = total.reshape(experts, cap, per * seg).astype(BF16)

    @pl.loop(1, experts)
    def _(i):
        row_copy(i, out3, in3, a_send, a_recv).wait_send()

    @pl.loop(0, experts)
    def _(n):
        i = row_order(n)

        @pl.when(i != 0)
        def _():
            row_copy(i, ret3, back3, b_send, b_recv).start()

    back3[me_e] = ret3[me_e]

    pl.loop(first_part, reps)(make_segment)

    def from_replica(k):
        dx, dy = offsets(k)
        return ((mx + nx - dx) % nx) * ny + (my + ny - dy) % ny

    block = 32
    lanes = hidden // 128

    @pl.loop(0, reps)
    def _(k):
        @pl.when(k != own_k)
        def _():
            seg_copy(k).wait_recv()

        r = from_replica(k)

        @pl.loop(0, k + 1)
        def _(j):
            s = from_replica(j)

            def add_block(n, total):
                at = pl.ds(pl.multiple_of(n * block, block), block)
                product = vbuf[r, at].astype(F32) * vbuf[s, at].astype(F32)
                for c in range(lanes):
                    column = product[:, c * 128 : (c + 1) * 128]
                    total = total + jnp.sum(column.reshape(block // 8, 8, 128), axis=0)
                return total

            total = lax.fori_loop(0, 3 * seg // block, add_block, jnp.zeros((8, 128), F32))
            acc[r * reps + s] = total
            acc[s * reps + r] = total

    lane = iota((reps, 128), 1)
    gram = jnp.zeros((reps, 128), F32)
    for r in range(reps):
        part = jnp.sum(acc[r * reps : (r + 1) * reps], axis=1)
        gram = gram + jnp.where(lane == r, jnp.sum(part, axis=1, keepdims=True), 0.0)
    gsend[...] = gram
    gbuf[me_r] = gram

    def gram_copy(i):
        to = (me_r + i) % reps
        return pltpu.make_async_remote_copy(
            src_ref=gsend, dst_ref=gbuf.at[me_r], send_sem=g_send.at[i], recv_sem=g_recv.at[i],
            device_id={"expert": me_e, "replica": to},
        )

    pl.loop(1, reps)(lambda i: gram_copy(i).start())

    @pl.loop(1, experts)
    def _(i):
        row_copy(i, ret3, back3, b_send, b_recv).wait_recv()

    flat_rows(back3)
    for c in range(0, width, cols):
        ig_ref[:, c : c + cols] = dot_rows(place[...], rows[:, c : c + cols]).astype(BF16)

    pl.loop(1, reps)(lambda i: gram_copy(i).wait_recv())
    total = gbuf[0]
    for r in range(1, reps):
        total = total + gbuf[r]
    gram = total[:, 0:reps]
    low, high = iota((reps, reps), 0), iota((reps, reps), 1)
    c_col = jnp.ones((reps, 1), F32)
    c_row = jnp.ones((1, reps), F32)
    for level in range(reps.bit_length() - 1):
        now = c_col * c_row * gram
        same = (low >> level) == (high >> level)
        pair = ((low >> (level + 1)) == (high >> (level + 1))) & jnp.logical_not(same)
        own = jnp.where(same, now, 0.0)
        other = jnp.where(pair, now, 0.0)
        own_row, own_col = jnp.sum(own, axis=0, keepdims=True), jnp.sum(own, axis=1, keepdims=True)
        ab_row, ab_col = jnp.sum(other, axis=0, keepdims=True), jnp.sum(other, axis=1, keepdims=True)
        norm_col = jnp.sum(jnp.where(same, own_row, 0.0), axis=1, keepdims=True)
        norm_row = jnp.sum(jnp.where(same, own_col, 0.0), axis=0, keepdims=True)
        cross_col = jnp.sum(jnp.where(same, ab_row, 0.0), axis=1, keepdims=True)
        cross_row = jnp.sum(jnp.where(same, ab_col, 0.0), axis=0, keepdims=True)
        c_col = c_col * (1.0 - cross_col / (2.0 * (norm_col + norm_eps)))
        c_row = c_row * (1.0 - cross_row / (2.0 * (norm_row + norm_eps)))

    coefs = [c_row[:, r : r + 1] for r in range(reps)]

    for m in range(3):

        @pl.loop(0, seg // 16)
        def _(n):
            src = pl.ds(pl.multiple_of(m * seg + n * 16, 16), 16)
            at = pl.ds(pl.multiple_of(n * 16, 16), 16)
            merged = jnp.zeros((16, hidden), F32)
            for r in range(reps):
                merged = merged + coefs[r] * vbuf[r, src].astype(F32)
            first = beta_first * fm_ref[m, at] + (1.0 - beta_first) * merged
            second = beta_second * sm_ref[m, at] + (1.0 - beta_second) * merged * merged
            step_ref[m, at] = first / first_fix / (jnp.sqrt(second / second_fix) + adam_eps)

    for c in ones + twos[0] + twos[1]:
        c.wait_send()

    @pl.loop(1, experts)
    def _(i):
        row_copy(i, ret3, back3, b_send, b_recv).wait_send()

    @pl.loop(0, reps)
    def _(k):
        @pl.when(k != own_k)
        def _():
            seg_copy(k).wait_send()

    pl.loop(1, reps)(lambda i: gram_copy(i).wait_send())


def grid_of(reps):
    ny = 1 << ((reps.bit_length() - 1) // 2)
    return reps // ny, ny


def shards(
    weights, first_moment, second_moment, out_grads, routes, task_ids, task_weights, saved_inputs
):
    experts = lax.axis_size("expert")
    reps = lax.axis_size("replica")
    nx, ny = grid_of(reps)
    row_count, width = out_grads.shape[1:]
    _, mats, seg, hidden = weights.shape
    slots = saved_inputs.shape[2]
    cap = slots // experts
    vmem = pl.BlockSpec(memory_space=pltpu.VMEM)
    smem = pl.BlockSpec(memory_space=pltpu.SMEM)
    dma = pltpu.SemaphoreType.DMA
    w_copies = 3 * (nx - 1 + ny - 1)
    input_grads, adam_step = pl.pallas_call(
        functools.partial(kernel, experts, nx, ny),
        out_shape=(
            jax.ShapeDtypeStruct((row_count, width), BF16),
            jax.ShapeDtypeStruct((mats, seg, hidden), F32),
        ),
        in_specs=[vmem, vmem, vmem, vmem, vmem, smem, smem, vmem],
        out_specs=(vmem, vmem),
        scratch_shapes=[
            pltpu.VMEM((slots, row_count), BF16),
            pltpu.VMEM((experts, cap, width), BF16),
            pltpu.VMEM((experts, cap, width), BF16),
            pltpu.VMEM((experts, cap, width), BF16),
            pltpu.VMEM((experts, cap, width), BF16),
            pltpu.VMEM((slots, width), BF16),
            pltpu.VMEM((mats, nx, ny, seg, hidden), BF16),
            pltpu.VMEM((slots, hidden), F32),
            pltpu.VMEM((slots, hidden), F32),
            pltpu.VMEM((slots, hidden), BF16),
            pltpu.VMEM((slots, hidden), BF16),
            pltpu.VMEM((slots, hidden), BF16),
            pltpu.VMEM((reps, mats * seg, hidden), BF16),
            pltpu.VMEM((reps, mats * seg, hidden), BF16),
            pltpu.VMEM((reps * reps, 8, 128), F32),
            pltpu.VMEM((reps, 128), F32),
            pltpu.VMEM((reps, reps, 128), F32),
            dma((experts,)), dma((experts,)), dma((experts,)), dma((experts,)),
            dma((w_copies,)), dma((w_copies,)),
            dma((reps,)), dma((reps,)), dma((reps,)), dma((reps,)),
        ],
        compiler_params=pltpu.CompilerParams(collective_id=0, has_side_effects=True),
        name="expert_step",
    )(
        weights[0], first_moment[0], second_moment[0], out_grads[0],
        routes.reshape(1, row_count), task_ids, task_weights, saved_inputs[0, 0],
    )
    return (input_grads[None], adam_step[None])


def solution(mesh):
    return jax.shard_map(
        shards,
        mesh=mesh,
        in_specs=(
            P("expert", None, "replica", None),
            P("expert", None, "replica", None),
            P("expert", None, "replica", None),
            P("replica", "expert", None),
            P("replica", "expert", None),
            P("replica", "expert"),
            P(),
            P("replica", "expert", None, None),
        ),
        out_specs=(P("replica", "expert", None), P("expert", None, "replica", None)),
        check_vma=False,
    )
```

time: 400 us -> 197 us (0.49)
  waiting for transfers between devices: 198 us -> 0 us
  Pallas kernels: 0 us -> 192 us
  starting transfers between devices: 67.8 us -> 0 us
  other arithmetic: 48.5 us -> 0 us
  between operations: 35 us -> 1.29 us
  matrix products: 26.6 us -> 0 us
  local copies, waits for them, and re-layouts: 22 us -> 2.84 us
    pallas_call x0 -> x1, Pallas kernels: none -> 192 us  [shards(): pl.pallas_call(functools.partial(kernel, experts, nx, ny), out_shape=(jax...]
    ppermute x14 -> x0, waiting for transfers between devices: 137 us -> none  [from_partner(): lax.ppermute(array, axis, [(i, i ^ 1 << bit) for i in range(lax.axis_size...]
    all_to_all x2 -> x0, waiting for transfers between devices: 56 us -> none  [the longest x1 56 us: shards(): lax.all_to_all(outgoing, 'expert', split_axis=0, concat_axis=0, tiled=True)]
    ppermute x14 -> x0, starting transfers between devices: 39.6 us -> none  [from_partner(): lax.ppermute(array, axis, [(i, i ^ 1 << bit) for i in range(lax.axis_size...]
    all_to_all x2 -> x0, starting transfers between devices: 28.2 us -> none  [the longest x1 15.5 us: shards(): lax.all_to_all(outgoing, 'expert', split_axis=0, concat_axis=0, tiled=True)]
    dot_general x10 -> x0, matrix products: 26.6 us -> none  [the longest x4 11.4 us: contract_rows(): lax.dot_general(left, right, (((0,), (0,)), ((), ())), preferred_element_...]
    add x14 -> x0, other arithmetic: 15.1 us -> none  [the longest x3 9.42 us: merge_level(): return kept_coef * kept_part + got_coef * got_part]
    another operation x6 -> x0, other arithmetic: 15 us -> none  [the longest x1 11.9 us: shards(): jnp.stack([contract_rows(inputs, gate_grad), contract_rows(inputs, up_gra...]
  transfers between devices with their start and end apart: 17 -> 0, of which waited for: 16 -> 0; matrix products, arithmetic and copies ran while one was open for 8% -> 0% of each run, Pallas kernels for 0% -> 0%
where the time goes in v1:
time: 197 us; the launch traced here: 196 us
  Pallas kernels  192 us (97%)
  local copies, waits for them, and re-layouts  2.84 us (1%)
    pallas_call x1, Pallas kernels, shards(): pl.pallas_call(functools.partial(kernel, experts, nx, ny), out_shape=(jax...  192 us

profile of v1, /device:TPU:6, one launch (start us, length us, event | category | flops | bytes accessed | tf_op | source)
XLA Modules:
  0.0 196.2 jit_solution(15849716668557095750)
XLA Ops:
  1.3 192.0 %expert_step.1 = (bf16[128,2048]{1,0:T(8,128)(2,1)}, f32[3,128,512]{2,1,0:T(8,128)}) custom-call(bf16[3,128,512]{2,1,0:T(8,128)(2,1)} %bitcast.14, f32[3,128,512]{2,1,0:T(8,128)} %bitcast.10, f32[3,128,512]{2,1,0:T(8,128)} %bitcast.11, bf16[128,2048]{1,0:T(8,128)(2,1)} %bitcast.13, s32[1,128]{1,0:T(1,128)} %bitcast.15, s32[1,1]{1,0:T(1,128)S(6)} %copy.12.tid_ref, ...), custom_call_target="tpu_custom_call" | custom-call | tf_op jit(solution)/shard_map/expert_step/pallas_call | solution.py:366
  193.3 0.0 copy-start
  193.3 2.0 copy.13
  195.3 0.0 copy-done
  195.3 0.9 copy.14
Async XLA Ops:
  193.3 2.0 %copy-start = (f32[3,128,512]{2,1,0:T(8,128)S(1)}, f32[3,128,512]{2,1,0:T(8,128)}, u32[]{:S(2)}) copy-start(f32[3,128,512]{2,1,0:T(8,128)} %get-tuple-element.5) | copy-start | bytes 2359300

commit v2 on v1

--- a/solution.py
+++ b/solution.py
@@ -169,44 +169,47 @@
             got = src[pl.ds(n * per, per)].astype(F32).reshape(16, width)
             rows[pl.ds(pl.multiple_of(n * 16, 16), 16)] = got.astype(BF16)
 
-    flat_rows(in3)
-    gact_now = jnp.dot(rows[...], weight(2), preferred_element_type=F32)
-    gg[...] = (gact_now * upfac[...]).astype(BF16)
-    ug[...] = (gact_now * gact[...]).astype(BF16)
+    order = sorted(
+        [(dx, dy) for dx in range(nx) for dy in range(ny)],
+        key=lambda o: (min(o[0], nx - o[0]) + min(o[1], ny - o[1]), o) if o != (0, 0) else (nx + ny, o),
+    )
+    code_x = sum(dx << (2 * k) for k, (dx, _) in enumerate(order))
+    code_y = sum(dy << (2 * k) for k, (_, dy) in enumerate(order))
+    own_k = reps - 1
 
     def offsets(k):
-        i, j = k // ny, k % ny
-        return (nx // 2 + (nx - 1) * i) % nx, (ny // 2 + (ny - 1) * j) % ny
-
-    own_k = (nx // 2) * ny + ny // 2
-
-    def seg_copy(k):
+        return (jnp.int32(code_x) >> (2 * k)) & 3, (jnp.int32(code_y) >> (2 * k)) & 3
+
+    def seg_copy(k, m):
         dx, dy = offsets(k)
         to = ((mx + dx) % nx) * ny + (my + dy) % ny
+        sem = m * reps + k
         return pltpu.make_async_remote_copy(
-            src_ref=vsend.at[to], dst_ref=vbuf.at[me_r], send_sem=v_send.at[k], recv_sem=v_recv.at[k],
+            src_ref=vsend.at[m, to], dst_ref=vbuf.at[m, me_r], send_sem=v_send.at[sem], recv_sem=v_recv.at[sem],
             device_id={"expert": me_e, "replica": to},
         )
 
-    def make_segment(k):
-        dx, dy = offsets(k)
-        to = ((mx + dx) % nx) * ny + (my + dy) % ny
-        at = pl.ds(pl.multiple_of(to * seg, seg), seg)
-        x_part = x_ref[:, at]
-        vsend[to, 0:seg] = dot_rows(x_part, gg[...]).astype(BF16)
-        vsend[to, seg : 2 * seg] = dot_rows(x_part, ug[...]).astype(BF16)
-        vsend[to, 2 * seg : 3 * seg] = dot_rows(rows[:, at], hid[...]).astype(BF16)
-
-        @pl.when(k != own_k)
-        def _():
-            seg_copy(k).start()
-
-        @pl.when(k == own_k)
-        def _():
-            vbuf[me_r] = vsend[me_r]
-
-    first_part = max(1, reps // 4)
-    pl.loop(0, first_part)(make_segment)
+    def make_segments(m, left, right):
+        @pl.loop(0, reps)
+        def _(k):
+            dx, dy = offsets(k)
+            to = ((mx + dx) % nx) * ny + (my + dy) % ny
+            at = pl.ds(pl.multiple_of(to * seg, seg), seg)
+            vsend[m, to] = dot_rows(left[:, at], right[...]).astype(BF16)
+
+            @pl.when(k != own_k)
+            def _():
+                seg_copy(k, m).start()
+
+            @pl.when(k == own_k)
+            def _():
+                vbuf[m, me_r] = vsend[m, me_r]
+
+    flat_rows(in3)
+    make_segments(2, rows, hid)
+    hidden_grad = jnp.dot(rows[...], weight(2), preferred_element_type=F32)
+    gg[...] = (hidden_grad * upfac[...]).astype(BF16)
+    ug[...] = (hidden_grad * gact[...]).astype(BF16)
 
     per = min(2, reps)
 
@@ -232,38 +235,42 @@
 
     back3[me_e] = ret3[me_e]
 
-    pl.loop(first_part, reps)(make_segment)
+    make_segments(0, x_ref, gg)
+    make_segments(1, x_ref, ug)
 
     def from_replica(k):
         dx, dy = offsets(k)
         return ((mx + nx - dx) % nx) * ny + (my + ny - dy) % ny
 
-    block = 32
     lanes = hidden // 128
-
-    @pl.loop(0, reps)
-    def _(k):
-        @pl.when(k != own_k)
-        def _():
-            seg_copy(k).wait_recv()
-
-        r = from_replica(k)
-
-        @pl.loop(0, k + 1)
-        def _(j):
-            s = from_replica(j)
-
-            def add_block(n, total):
-                at = pl.ds(pl.multiple_of(n * block, block), block)
-                product = vbuf[r, at].astype(F32) * vbuf[s, at].astype(F32)
-                for c in range(lanes):
-                    column = product[:, c * 128 : (c + 1) * 128]
-                    total = total + jnp.sum(column.reshape(block // 8, 8, 128), axis=0)
-                return total
-
-            total = lax.fori_loop(0, 3 * seg // block, add_block, jnp.zeros((8, 128), F32))
-            acc[r * reps + s] = total
-            acc[s * reps + r] = total
+    acc[...] = jnp.zeros_like(acc)
+
+    @pl.loop(0, 3)
+    def _(n):
+        m = (n + 2) % 3
+
+        @pl.loop(0, reps)
+        def _(k):
+            @pl.when(k != own_k)
+            def _():
+                seg_copy(k, m).wait_recv()
+
+            r = from_replica(k)
+
+            @pl.loop(0, k + 1)
+            def _(j):
+                s = from_replica(j)
+                sums = [acc[r * reps + s]] + [jnp.zeros((8, 128), F32)] * (lanes - 1)
+                for i in range(0, seg, 16):
+                    product = vbuf[m, r, i : i + 16].astype(F32) * vbuf[m, s, i : i + 16].astype(F32)
+                    for c in range(lanes):
+                        column = product[:, c * 128 : (c + 1) * 128]
+                        sums[c] = sums[c] + column[0:8] + column[8:16]
+                total = sums[0]
+                for c in range(1, lanes):
+                    total = total + sums[c]
+                acc[r * reps + s] = total
+                acc[s * reps + r] = total
 
     lane = iota((reps, 128), 1)
     gram = jnp.zeros((reps, 128), F32)
@@ -319,11 +326,10 @@
 
         @pl.loop(0, seg // 16)
         def _(n):
-            src = pl.ds(pl.multiple_of(m * seg + n * 16, 16), 16)
             at = pl.ds(pl.multiple_of(n * 16, 16), 16)
             merged = jnp.zeros((16, hidden), F32)
             for r in range(reps):
-                merged = merged + coefs[r] * vbuf[r, src].astype(F32)
+                merged = merged + coefs[r] * vbuf[m, r, at].astype(F32)
             first = beta_first * fm_ref[m, at] + (1.0 - beta_first) * merged
             second = beta_second * sm_ref[m, at] + (1.0 - beta_second) * merged * merged
             step_ref[m, at] = first / first_fix / (jnp.sqrt(second / second_fix) + adam_eps)
@@ -339,7 +345,8 @@
     def _(k):
         @pl.when(k != own_k)
         def _():
-            seg_copy(k).wait_send()
+            for m in range(3):
+                seg_copy(k, m).wait_send()
 
     pl.loop(1, reps)(lambda i: gram_copy(i).wait_send())
 
@@ -384,14 +391,14 @@
             pltpu.VMEM((slots, hidden), BF16),
             pltpu.VMEM((slots, hidden), BF16),
             pltpu.VMEM((slots, hidden), BF16),
-            pltpu.VMEM((reps, mats * seg, hidden), BF16),
-            pltpu.VMEM((reps, mats * seg, hidden), BF16),
+            pltpu.VMEM((mats, reps, seg, hidden), BF16),
+            pltpu.VMEM((mats, reps, seg, hidden), BF16),
             pltpu.VMEM((reps * reps, 8, 128), F32),
             pltpu.VMEM((reps, 128), F32),
             pltpu.VMEM((reps, reps, 128), F32),
             dma((experts,)), dma((experts,)), dma((experts,)), dma((experts,)),
             dma((w_copies,)), dma((w_copies,)),
-            dma((reps,)), dma((reps,)), dma((reps,)), dma((reps,)),
+            dma((mats * reps,)), dma((mats * reps,)), dma((reps,)), dma((reps,)),
         ],
         compiler_params=pltpu.CompilerParams(collective_id=0, has_side_effects=True),
         name="expert_step",

time: 197 us -> 169 us (0.86)
  the two profiles are of different devices: /device:TPU:6 before, /device:TPU:192 now
where the time goes in v2:
time: 169 us; the launch traced here: 168 us
  Pallas kernels  164 us (97%)
  local copies, waits for them, and re-layouts  2.84 us (2%)
    pallas_call x1, Pallas kernels, shards(): pl.pallas_call(functools.partial(kernel, experts, nx, ny), out_shape=(jax...  164 us

profile of v2, /device:TPU:192, one launch (start us, length us, event | category | flops | bytes accessed | tf_op | source)
XLA Modules:
  0.0 168.5 jit_solution(154361180192248692)
XLA Ops:
  1.3 164.4 %expert_step.1 = (bf16[128,2048]{1,0:T(8,128)(2,1)}, f32[3,128,512]{2,1,0:T(8,128)}) custom-call(bf16[3,128,512]{2,1,0:T(8,128)(2,1)} %bitcast.14, f32[3,128,512]{2,1,0:T(8,128)} %bitcast.10, f32[3,128,512]{2,1,0:T(8,128)} %bitcast.11, bf16[128,2048]{1,0:T(8,128)(2,1)} %bitcast.13, s32[1,128]{1,0:T(1,128)} %bitcast.15, s32[1,1]{1,0:T(1,128)S(6)} %copy.12.tid_ref, ...), custom_call_target="tpu_custom_call" | custom-call | tf_op jit(solution)/shard_map/expert_step/pallas_call | solution.py:373
  165.6 0.0 copy-start
  165.7 2.0 %copy.13 = bf16[1,128,2048]{2,1,0:T(8,128)(2,1)} copy(bf16[1,128,2048]{2,1,0:T(8,128)(2,1)} %bitcast.12) | data formatting | bytes 1048576
  167.6 0.0 copy-done
  167.6 0.9 copy.14
Async XLA Ops:
  165.6 2.0 %copy-start = (f32[3,128,512]{2,1,0:T(8,128)S(1)}, f32[3,128,512]{2,1,0:T(8,128)}, u32[]{:S(2)}) copy-start(f32[3,128,512]{2,1,0:T(8,128)} %get-tuple-element.5) | copy-start | bytes 2359300
